TPU v7x, 32 devices: a whole 2x2x4 slice. The times are simulated.
32 devices in a mesh: gz: 2 (over y), row: 4 (over x, core), col: 4 (over z).
Axes of the slice: x: 2, y: 2, z: 4, core: 2. Of those that a mesh axis runs over, the one named last changes fastest.
Arguments:
- anc_lower: bfloat16 [1, 1024, 1024], P(None, 'col', 'row'), may hold values from -0.125 to 0.125
- anc_upper: bfloat16 [1, 1024, 1024], P(None, 'col', 'row'), may hold values from -0.125 to 0.125
- sub_lower: bfloat16 [16, 1024, 1024], P('gz', 'col', 'row'), may hold values from -0.125 to 0.125
- sub_upper: bfloat16 [16, 1024, 1024], P('gz', 'col', 'row'), may hold values from -0.125 to 0.125
- anc_rhs: bfloat16 [1, 1024, 64], P(None, 'col'), may hold values from -6 to 6
- sub_rhs: bfloat16 [6, 1024, 64], P('gz', 'col'), may hold values from -6 to 6
- layer_subtree: int32 [2], replicated, may hold values from 0 to 1, each once
- sub_pattern: int32 [10, 2], P('gz'), may hold values 0 or 1
Outputs:
- anc_solution: float32 [1, 1024, 64], P(None, ('row', 'col'))
- sub_solution: float32 [6, 1024, 64], P('gz', ('row', 'col'))
Inputs may be any that keep to these rules, and one draw needn't show every extreme that they name: `layer_subtree`: each subtree is held by exactly one layer.
All inputs are finite; a program needn't handle non-finite values. No bound on the sum of `sub_pattern` on one device may be relied on, other than what follows from the above.
Results may differ from a plain program's by a relative error of at most 0.018.
Values may be sent and summed in bfloat16 or wider, within the bound.
A program may use at most 64 MiB of HBM per device.

v0:
```python
import jax
import jax.numpy as jnp
import numpy as np
from jax import lax
from jax.sharding import PartitionSpec as P

R = 64
SUB_LEVELS = 2
SUB_NODES = 3


def level_span(depth_now):
    return (2**depth_now - 1, 2 ** (depth_now + 1) - 1)


def local_routes(first_id, stop_id, depth_now, target_count):
    table = np.zeros((target_count, (stop_id - first_id) * depth_now), np.float32)
    for offset, member in enumerate(range(first_id, stop_id)):
        for local_level in range(depth_now):
            target = (member + 1 >> depth_now - local_level) - 1
            table[target, offset * depth_now + local_level] = 1.0
    return table


def solve_diagonal(residual, blocks):
    whole_blocks = lax.all_gather(blocks, "col", axis=1, tiled=True)
    whole_res = lax.all_gather(residual, "col", axis=1, tiled=True)
    rows_full = jnp.einsum(
        "nki,nkr->nir", whole_blocks, whole_res, preferred_element_type=jnp.float32
    )
    share = rows_full.shape[1] // lax.axis_size("col")
    owned = lax.dynamic_slice_in_dim(rows_full, lax.axis_index("col") * share, share, 1)
    return (owned, rows_full.astype(jnp.bfloat16))


def upper_sum(values):
    return lax.psum(values, "row")


def local(anc_lower, anc_upper, sub_lower, sub_upper, anc_rhs, sub_rhs, layer_subtree, sub_pattern):
    layers = lax.axis_size("gz")
    levels = layers.bit_length() - 1
    anc_count = layers - 1
    row_count = lax.axis_size("row")
    col_count = lax.axis_size("col")
    rows_here = anc_lower.shape[2]
    cols_here = anc_lower.shape[1]
    sub_start = [0]
    for member in range(SUB_NODES):
        sub_start.append(sub_start[-1] + levels + (member + 1).bit_length() - 1)
    anc_start = [0]
    for member in range(anc_count):
        anc_start.append(anc_start[-1] + (member + 1).bit_length() - 1)
    low_pattern = sub_pattern[:, 0].astype(jnp.float32)
    up_pattern = sub_pattern[:, 1].astype(jnp.float32)
    layer_here = lax.axis_index("gz")
    subtree = jnp.sum(
        jnp.where(jnp.arange(layers, dtype=jnp.int32) == layer_here, layer_subtree, 0)
    )
    powers = jnp.asarray(2 ** (levels - np.arange(levels)), jnp.int32)
    heap_ids = (subtree + layers) // powers - 1
    choose = (heap_ids[:, None] == jnp.arange(anc_count, dtype=jnp.int32)[None, :]).astype(
        jnp.float32
    )
    first_layer = (layer_here == 0).astype(jnp.float32)
    row_index = lax.axis_index("row")
    col_index = lax.axis_index("col")
    holds_piece = (row_index == col_index * row_count // col_count).astype(jnp.float32)
    piece_start = jnp.clip(col_index * cols_here - row_index * rows_here, 0, rows_here - cols_here)

    def own_piece(rows_block):
        return holds_piece * lax.dynamic_slice_in_dim(rows_block, piece_start, cols_here, 1).astype(
            jnp.float32
        )

    sub_acc = jnp.zeros((SUB_NODES, cols_here, R), jnp.float32)
    to_anc = jnp.zeros((anc_count, cols_here, R), jnp.float32)
    sub_rows = {}
    for depth_now in reversed(range(SUB_LEVELS)):
        first_id, stop_id = level_span(depth_now)
        node_count = stop_id - first_id
        given = sub_rhs[first_id:stop_id].astype(jnp.float32)
        if depth_now + 1 < SUB_LEVELS:
            given = given - lax.psum(sub_acc[first_id:stop_id], "row")
        unused, solved = solve_diagonal(given.astype(jnp.bfloat16), sub_lower[first_id:stop_id])
        sub_rows[depth_now] = solved
        per_node = levels + depth_now
        opening = SUB_NODES + sub_start[first_id]
        blocks = sub_lower[opening : opening + node_count * per_node].reshape(
            node_count, per_node, cols_here, rows_here
        )
        weights = low_pattern[sub_start[first_id] : sub_start[stop_id]].reshape(
            node_count, per_node
        )
        updates = jnp.einsum("npik,nkr->npir", blocks, solved, preferred_element_type=jnp.float32)
        updates = updates * weights[:, :, None, None]
        to_anc = to_anc + jnp.einsum("ea,eir->air", choose, jnp.sum(updates[:, :levels], 0))
        if depth_now > 0:
            table = jnp.asarray(local_routes(first_id, stop_id, depth_now, SUB_NODES))
            sub_acc = sub_acc + jnp.einsum(
                "tq,qir->tir", table, updates[:, levels:].reshape(-1, cols_here, R)
            )
    anc_acc = jnp.zeros((anc_count, cols_here, R), jnp.float32)
    anc_rows = {}
    for depth_now in reversed(range(levels)):
        first_id, stop_id = level_span(depth_now)
        node_count = stop_id - first_id
        joined = to_anc[first_id:stop_id] + first_layer * anc_acc[first_id:stop_id]
        reached = lax.psum(joined, ("gz", "row"))
        given = anc_rhs[first_id:stop_id].astype(jnp.float32) - reached
        unused, solved = solve_diagonal(given.astype(jnp.bfloat16), anc_lower[first_id:stop_id])
        anc_rows[depth_now] = solved
        if depth_now > 0:
            opening = anc_count + anc_start[first_id]
            blocks = anc_lower[opening : opening + node_count * depth_now].reshape(
                node_count, depth_now, cols_here, rows_here
            )
            updates = jnp.einsum(
                "npik,nkr->npir", blocks, solved, preferred_element_type=jnp.float32
            )
            table = jnp.asarray(local_routes(first_id, stop_id, depth_now, anc_count))
            anc_acc = anc_acc + jnp.einsum("tq,qir->tir", table, updates.reshape(-1, cols_here, R))
    anc_z_parts = []
    anc_out_parts = []
    for depth_now in range(levels):
        first_id, stop_id = level_span(depth_now)
        node_count = stop_id - first_id
        given = own_piece(anc_rows[depth_now])
        if depth_now > 0:
            z_sofar = jnp.concatenate(anc_z_parts, 0)
            table = local_routes(first_id, stop_id, depth_now, anc_count)[:first_id].T
            sources = jnp.einsum(
                "qa,akr->qkr",
                jnp.asarray(table, jnp.bfloat16),
                z_sofar,
                preferred_element_type=jnp.float32,
            )
            sources = sources.astype(jnp.bfloat16).reshape(node_count, depth_now, rows_here, R)
            opening = anc_count + anc_start[first_id]
            blocks = anc_upper[opening : opening + node_count * depth_now].reshape(
                node_count, depth_now, cols_here, rows_here
            )
            updates = jnp.einsum(
                "npik,npkr->npir", blocks, sources, preferred_element_type=jnp.float32
            )
            given = given - jnp.sum(updates, 1)
        summed = upper_sum(given)
        owned, solved = solve_diagonal(summed.astype(jnp.bfloat16), anc_upper[first_id:stop_id])
        anc_out_parts.append(owned)
        anc_z_parts.append(solved)
    anc_z_all = jnp.concatenate(anc_z_parts, 0)
    selected = jnp.einsum(
        "ea,akr->ekr", choose.astype(jnp.bfloat16), anc_z_all, preferred_element_type=jnp.float32
    )
    selected = selected.astype(jnp.bfloat16)
    sub_z_parts = []
    sub_out_parts = []
    for depth_now in range(SUB_LEVELS):
        first_id, stop_id = level_span(depth_now)
        node_count = stop_id - first_id
        per_node = levels + depth_now
        opening = SUB_NODES + sub_start[first_id]
        blocks = sub_upper[opening : opening + node_count * per_node].reshape(
            node_count, per_node, cols_here, rows_here
        )
        weights = up_pattern[sub_start[first_id] : sub_start[stop_id]].reshape(node_count, per_node)
        updates = jnp.einsum(
            "npik,pkr->npir", blocks[:, :levels], selected, preferred_element_type=jnp.float32
        )
        if depth_now > 0:
            z_sofar = sub_z_parts[0]
            table = local_routes(first_id, stop_id, depth_now, SUB_NODES)[:first_id].T
            sources = jnp.einsum(
                "qa,akr->qkr",
                jnp.asarray(table, jnp.bfloat16),
                z_sofar,
                preferred_element_type=jnp.float32,
            )
            sources = sources.astype(jnp.bfloat16).reshape(node_count, depth_now, rows_here, R)
            local_updates = jnp.einsum(
                "npik,npkr->npir", blocks[:, levels:], sources, preferred_element_type=jnp.float32
            )
            updates = jnp.concatenate([updates, local_updates], 1)
        change = jnp.sum(updates * weights[:, :, None, None], 1)
        summed = upper_sum(own_piece(sub_rows[depth_now]) - change)
        owned, solved = solve_diagonal(summed.astype(jnp.bfloat16), sub_upper[first_id:stop_id])
        sub_out_parts.append(owned)
        sub_z_parts.append(solved)
    return (jnp.concatenate(anc_out_parts, 0), jnp.concatenate(sub_out_parts, 0))


def solution(mesh):
    in_specs = (
        P(None, "col", "row"),
        P(None, "col", "row"),
        P("gz", "col", "row"),
        P("gz", "col", "row"),
        P(None, "col", None),
        P("gz", "col", None),
        P(),
        P("gz", None),
    )
    out_specs = (P(None, ("row", "col"), None), P("gz", ("row", "col"), None))
    return jax.shard_map(local, mesh=mesh, in_specs=in_specs, out_specs=out_specs, check_vma=False)
```

profile of v0, /device:TPU:0, one launch (start us, length us, event | category | flops | bytes accessed | tf_op | source)
XLA Modules:
  0.0 251.9 jit_solution(8480645708661849595)
XLA Ops:
  7.2 1.7 slice.67
  9.0 0.6 copy-done.7
  9.6 0.6 fusion.35
  11.0 0.7 copy-done.6
  11.8 17.3 %all_gather.37 = bf16[2,1024,64]{1,2,0:T(8,128)(2,1)S(1)} all-gather(bf16[2,256,64]{1,2,0:T(8,128)(2,1)S(1)} %slice-done.3), channel_id=1, replica_groups=mesh['gz'=2,'row'=4,'col'=4] {'col'}, dimensions={1}, use_global_device_ids=true | all-gather | bytes 327680 | tf_op jit(solution)/shard_map/all_gather | solution.py:27
  29.1 22.6 %all_gather.39 = bf16[1,1024,256]{2,1,0:T(8,128)(2,1)S(1)} all-gather(bf16[1,256,256]{2,1,0:T(8,128)(2,1)S(1)} %slice-done.1), channel_id=1, replica_groups=mesh['gz'=2,'row'=4,'col'=4] {'col'}, dimensions={1}, use_global_device_ids=true | all-gather | bytes 655360 | tf_op jit(solution)/shard_map/all_gather | solution.py:26
  51.7 1.6 convolution_convert_fusion
  53.4 0.3 fusion
  53.7 0.3 copy-done.8
  54.0 0.9 fusion.27
  55.0 30.0 %all-reduce.4.cloned.1.call-done = f32[1,256,64]{1,0,2:T(1,128)} async-done(((f32[1,256,64]{1,0,2:T(1,128)}), f32[1,256,64]{1,0,2:T(1,128)}) %all-reduce.4.cloned.1.call-update) | async-done | bytes 65552 | tf_op jit(solution)/shard_map/psum | solution.py:84
  85.0 0.9 fusion.30
  85.9 13.5 %all_gather.38 = bf16[1,1024,64]{1,0,2:T(2,128)(2,1)S(1)} all-gather(bf16[1,256,64]{1,0,2:T(2,128)(2,1)S(1)} %fusion.30), channel_id=1, replica_groups=mesh['gz'=2,'row'=4,'col'=4] {'col'}, dimensions={1}, use_global_device_ids=true | all-gather | bytes 163840 | tf_op jit(solution)/shard_map/all_gather | solution.py:27
  99.4 0.2 convolution_convert_fusion.2
  99.6 0.9 fusion.7
  100.5 0.7 slice.87
  101.4 0.8 copy-done.3
  102.2 14.9 %all_gather.41 = bf16[1,1024,256]{2,1,0:T(8,128)(2,1)S(1)} all-gather(bf16[1,256,256]{2,1,0:T(8,128)(2,1)S(1)} %copy-done.3), channel_id=1, replica_groups=mesh['gz'=2,'row'=4,'col'=4] {'col'}, dimensions={1}, use_global_device_ids=true | all-gather | bytes 655360 | tf_op jit(solution)/shard_map/all_gather | solution.py:26
  117.1 16.3 %all_gather.43 = bf16[1,1024,256]{2,1,0:T(8,128)(2,1)S(1)} all-gather(bf16[1,256,256]{2,1,0:T(8,128)(2,1)S(1)} %copy-done.4), channel_id=1, replica_groups=mesh['gz'=2,'row'=4,'col'=4] {'col'}, dimensions={1}, use_global_device_ids=true | all-gather | bytes 655360 | tf_op jit(solution)/shard_map/all_gather | solution.py:26
  133.4 14.8 %all_gather.45 = bf16[1,1024,256]{2,1,0:T(8,128)(2,1)S(1)} all-gather(bf16[1,256,256]{2,1,0:T(8,128)(2,1)S(1)} %slice-done.2), channel_id=1, replica_groups=mesh['gz'=2,'row'=4,'col'=4] {'col'}, dimensions={1}, use_global_device_ids=true | all-gather | bytes 655360 | tf_op jit(solution)/shard_map/all_gather | solution.py:26
  148.5 2.8 %all-reduce.6.cloned.1.call-done = f32[1,256,64]{1,2,0:T(8,128)} async-done(((f32[1,256,64]{1,2,0:T(8,128)}), f32[1,256,64]{1,2,0:T(8,128)}) %all-reduce.6.cloned.1.call-update) | async-done | bytes 65552 | tf_op jit(solution)/shard_map/psum | solution.py:109
  151.3 0.8 subtract_convert_fusion
  152.1 13.9 %all_gather.40 = bf16[1,1024,64]{1,2,0:T(8,128)(2,1)S(1)} all-gather(bf16[1,256,64]{1,2,0:T(8,128)(2,1)S(1)} %subtract_convert_fusion), channel_id=1, replica_groups=mesh['gz'=2,'row'=4,'col'=4] {'col'}, dimensions={1}, use_global_device_ids=true | all-gather | bytes 163840 | tf_op jit(solution)/shard_map/all_gather | solution.py:27
  166.2 11.5 %psum.37 = bf16[1,256,64]{1,2,0:T(8,128)(2,1)S(1)} all-reduce(f32[1,256,64]{1,2,0:T(8,128)S(1)} %fusion.10), channel_id=1, replica_groups=mesh['gz'=2,'row'=4,'col'=4] {'row'}, use_global_device_ids=true, to_apply=%region_4.5 | all-reduce | flops 16384 | bytes 98304 | tf_op jit(solution)/shard_map/psum | solution.py:37
  177.7 13.4 %all_gather.42 = bf16[1,1024,64]{1,2,0:T(8,128)(2,1)S(1)} all-gather(bf16[1,256,64]{1,2,0:T(8,128)(2,1)S(1)} %psum.37), channel_id=1, replica_groups=mesh['gz'=2,'row'=4,'col'=4] {'col'}, dimensions={1}, use_global_device_ids=true | all-gather | bytes 163840 | tf_op jit(solution)/shard_map/all_gather | solution.py:27
  191.5 10.7 %psum.38 = bf16[1,256,64]{1,2,0:T(8,128)(2,1)S(1)} all-reduce(f32[1,256,64]{1,2,0:T(8,128)S(1)} %fusion.3), channel_id=1, replica_groups=mesh['gz'=2,'row'=4,'col'=4] {'row'}, use_global_device_ids=true, to_apply=%region_5.6 | all-reduce | flops 16384 | bytes 98304 | tf_op jit(solution)/shard_map/psum | solution.py:37
  202.2 13.3 %all_gather.44 = bf16[1,1024,64]{1,2,0:T(8,128)(2,1)S(1)} all-gather(bf16[1,256,64]{1,2,0:T(8,128)(2,1)S(1)} %psum.38), channel_id=1, replica_groups=mesh['gz'=2,'row'=4,'col'=4] {'col'}, dimensions={1}, use_global_device_ids=true | all-gather | bytes 163840 | tf_op jit(solution)/shard_map/all_gather | solution.py:27
  216.3 11.9 %all-reduce.7 = bf16[2,256,64]{1,2,0:T(8,128)(2,1)S(1)} all-reduce(f32[2,256,64]{1,2,0:T(8,128)S(1)} %multiply_subtract_fusion), channel_id=1, replica_groups=mesh['gz'=2,'row'=4,'col'=4] {'row'}, use_global_device_ids=true, to_apply=%region_7.8 | all-reduce | flops 32768 | bytes 196608 | tf_op jit(solution)/shard_map/psum | solution.py:37
  228.2 14.0 %all_gather.46 = bf16[2,1024,64]{1,2,0:T(8,128)(2,1)S(1)} all-gather(bf16[2,256,64]{1,2,0:T(8,128)(2,1)S(1)} %all-reduce.7), channel_id=1, replica_groups=mesh['gz'=2,'row'=4,'col'=4] {'col'}, dimensions={1}, use_global_device_ids=true | all-gather | bytes 327680 | tf_op jit(solution)/shard_map/all_gather | solution.py:27
  242.3 1.5 fusion.36
  243.9 0.7 copy.24
  244.7 0.7 copy.23
  (56 shorter events, 2.4 us)
Async XLA Ops:
  7.2 44.6 %all-gather.3.cloned.1.call-start = ((), (), s32[]{:S(2)}) async-start(), calls=%async_computation | async-start | bytes 1310720 | tf_op jit(solution)/shard_map/all_gather | solution.py:26
  8.9 76.1 %all-reduce.4.cloned.1.call-start = ((), (), s32[]{:S(2)}) async-start(), calls=%async_computation.1 | async-start | bytes 131072 | tf_op jit(solution)/shard_map/psum | solution.py:84
  9.0 0.7 copy-start.7
  10.9 0.9 slice-start.3
  10.9 0.7 copy-start.6
  11.8 17.3 %slice-start.1 = ((bf16[8,256,256]{2,1,0:T(8,128)(2,1)}), bf16[1,256,256]{2,1,0:T(8,128)(2,1)S(1)}, s32[]{:S(2)}) async-start(bf16[8,256,256]{2,1,0:T(8,128)(2,1)} %param.13), calls=%async_computation.5 | async-start | bytes 262144 | tf_op jit(solution)/shard_map/slice | solution.py:85
  51.7 1.6 slice-start
  53.3 0.7 copy-start.8
  53.3 31.7 %slice-start.4 = ((bf16[3,256,64]{1,2,0:T(8,128)(2,1)}), bf16[1,256,64]{1,2,0:T(8,128)(2,1)S(1)}, s32[]{:S(2)}) async-start(bf16[3,256,64]{1,2,0:T(8,128)(2,1)} %param.16), calls=%async_computation.8 | async-start | bytes 65536 | tf_op jit(solution)/shard_map/slice | solution.py:82
  53.6 46.0 %copy-start = (bf16[8,256,256]{2,1,0:T(8,128)(2,1)S(1)}, bf16[8,256,256]{2,1,0:T(8,128)(2,1)}, u32[]{:S(2)}) copy-start(bf16[8,256,256]{2,1,0:T(8,128)(2,1)} %param.13) | copy-start | bytes 3145732
  54.0 46.5 %copy-start.1 = (bf16[8,256,256]{2,1,0:T(8,128)(2,1)S(1)}, bf16[8,256,256]{2,1,0:T(8,128)(2,1)}, u32[]{:S(2)}) copy-start(bf16[8,256,256]{2,1,0:T(8,128)(2,1)} %param.14) | copy-start | bytes 3145732
  54.9 96.3 %all-reduce.6.cloned.1.call-start = ((), (), s32[]{:S(2)}) async-start(), calls=%async_computation.2 | async-start | bytes 131072 | tf_op jit(solution)/shard_map/psum | solution.py:109
  100.5 141.8 %all-gather.5.cloned.1.call-start = ((), (), s32[]{:S(2)}) async-start(), calls=%async_computation.3 | async-start | bytes 1310720 | tf_op jit(solution)/shard_map/all_gather | solution.py:26
  101.3 0.9 copy-start.3
  102.2 14.9 %copy-start.4 = (bf16[1,256,256]{2,1,0:T(8,128)(2,1)S(1)}, bf16[1,256,256]{2,1,0:T(8,128)(2,1)}, u32[]{:S(2)}) copy-start(bf16[1,256,256]{2,1,0:T(8,128)(2,1)} %param.12) | copy-start | bytes 393220
  117.1 16.3 %slice-start.2 = ((bf16[8,256,256]{2,1,0:T(8,128)(2,1)}), bf16[1,256,256]{2,1,0:T(8,128)(2,1)S(1)}, s32[]{:S(2)}) async-start(bf16[8,256,256]{2,1,0:T(8,128)(2,1)} %param.14), calls=%async_computation.6 | async-start | bytes 262144 | tf_op jit(solution)/shard_map/slice | solution.py:186
  133.4 17.9 %copy-start.5 = (bf16[1,256,64]{1,2,0:T(8,128)(2,1)S(1)}, bf16[1,256,64]{1,2,0:T(8,128)(2,1)}, u32[]{:S(2)}) copy-start(bf16[1,256,64]{1,2,0:T(8,128)(2,1)} %param.15) | copy-start | bytes 98308
  148.2 43.1 %copy-start.2 = (bf16[8,256,256]{2,1,0:T(8,128)(2,1)S(1)}, bf16[8,256,256]{2,1,0:T(8,128)(2,1)}, u32[]{:S(2)}) copy-start(bf16[8,256,256]{2,1,0:T(8,128)(2,1)} %param.14) | copy-start | bytes 3145732
Sparse Core Ops, SparseCore 0:
  9.5 40.4 all-gather.2
  55.0 29.9 all-reduce.3
  100.6 50.5 all-reduce.5
  152.7 27.7 all-gather.4
where the time goes:
time: 253 us; the launch traced here: 252 us
  blocking collectives  188 us (74%)
  waiting for transfers between devices  32.9 us (13%)
  between operations  14.7 us (6%)
  local copies, waits for them, and re-layouts  7.11 us (3%)
  matrix products  6.59 us (3%)
    all_gather x6, blocking collectives, solve_diagonal(): whole_res = lax.all_gather(residual, 'col', axis=1, tiled=True)  85.3 us
    all_gather x4, blocking collectives, solve_diagonal(): whole_blocks = lax.all_gather(blocks, 'col', axis=1, tiled=True)  68.6 us
    psum x3, blocking collectives, upper_sum(): return lax.psum(values, 'row')  34 us
    psum x1, waiting for transfers between devices, local(): given = given - lax.psum(sub_acc[first_id:stop_id], 'row')  30 us
  transfers between devices with their start and end apart: 4, of which 2 were waited for; matrix products, arithmetic and copies ran while one was open for 2% of the time, Pallas kernels for 0%

commit v1 on v0

--- a/solution.py
+++ b/solution.py
@@ -23,11 +23,38 @@
 
 
 def solve_diagonal(residual, blocks):
-    whole_blocks = lax.all_gather(blocks, "col", axis=1, tiled=True)
     whole_res = lax.all_gather(residual, "col", axis=1, tiled=True)
+    length, index, rows = (lax.axis_size("col"), lax.axis_index("col"), blocks.shape[1])
+    right = [(i, (i + 1) % length) for i in range(length)]
+    behind = [(i, (i - 1) % length) for i in range(length)]
+    half = length // 2
+    from_left = from_right = blocks
     rows_full = jnp.einsum(
-        "nki,nkr->nir", whole_blocks, whole_res, preferred_element_type=jnp.float32
-    )
+        "nki,nkr->nir",
+        blocks,
+        lax.dynamic_slice_in_dim(whole_res, index * rows, blocks.shape[1], axis=1),
+        preferred_element_type=jnp.float32,
+    )
+    for step in range(1, half + 1):
+        from_left = lax.ppermute(from_left, "col", right)
+        if step < length - half:
+            from_right = lax.ppermute(from_right, "col", behind)
+            rows_full = rows_full + jnp.einsum(
+                "nki,nkr->nir",
+                from_right,
+                lax.dynamic_slice_in_dim(
+                    whole_res, (index + step) % length * rows, from_right.shape[1], axis=1
+                ),
+                preferred_element_type=jnp.float32,
+            )
+        rows_full = rows_full + jnp.einsum(
+            "nki,nkr->nir",
+            from_left,
+            lax.dynamic_slice_in_dim(
+                whole_res, (index - step) % length * rows, from_left.shape[1], axis=1
+            ),
+            preferred_element_type=jnp.float32,
+        )
     share = rows_full.shape[1] // lax.axis_size("col")
     owned = lax.dynamic_slice_in_dim(rows_full, lax.axis_index("col") * share, share, 1)
     return (owned, rows_full.astype(jnp.bfloat16))

time: 253 us -> 294 us (1.16)
  waiting for transfers between devices: 32.9 us -> 111 us
  blocking collectives: 188 us -> 121 us
  starting transfers between devices: 0.16 us -> 22.7 us
  matrix products: 6.59 us -> 14.5 us
    all_gather x4 -> x0, blocking collectives: 68.6 us -> none  [solve_diagonal(): whole_blocks = lax.all_gather(blocks, 'col', axis=1, tiled=True)]
    psum x1, waiting for transfers between devices: 2.79 us -> 51.9 us  [local(): reached = lax.psum(joined, ('gz', 'row'))]
    ppermute x0 -> x18, waiting for transfers between devices: none -> 29.1 us  [the longest x12 29.1 us: solve_diagonal(): from_left = lax.ppermute(from_left, 'col', right)]
    ppermute x0 -> x18, starting transfers between devices: none -> 22.6 us  [the longest x6 17.1 us: solve_diagonal(): from_right = lax.ppermute(from_right, 'col', behind)]
    dot_general x6 -> x24, matrix products: 3.94 us -> 11.8 us  [the longest x12 5.52 us: solve_diagonal(): jnp.einsum('nki,nkr->nir', from_left, lax.dynamic_slice_in_dim(whole_res,...]
  transfers between devices with their start and end apart: 4 -> 20, of which waited for: 2 -> 6; matrix products, arithmetic and copies ran while one was open for 2% -> 7% of each run, Pallas kernels for 0% -> 0%
where the time goes in v1:
time: 294 us; the launch traced here: 293 us
  blocking collectives  121 us (41%)
  waiting for transfers between devices  111 us (38%)
  starting transfers between devices  22.7 us (8%)
  between operations  15 us (5%)
  matrix products  14.5 us (5%)
  local copies, waits for them, and re-layouts  5.82 us (2%)
    all_gather x6, blocking collectives, solve_diagonal(): whole_res = lax.all_gather(residual, 'col', axis=1, tiled=True)  88.1 us
    psum x1, waiting for transfers between devices, local(): reached = lax.psum(joined, ('gz', 'row'))  51.9 us
    psum x3, blocking collectives, upper_sum(): return lax.psum(values, 'row')  33.1 us
    psum x1, waiting for transfers between devices, local(): given = given - lax.psum(sub_acc[first_id:stop_id], 'row')  30 us
    ppermute x12, waiting for transfers between devices, solve_diagonal(): from_left = lax.ppermute(from_left, 'col', right)  29.1 us
    ppermute x6, starting transfers between devices, solve_diagonal(): from_right = lax.ppermute(from_right, 'col', behind)  17.1 us
  transfers between devices with their start and end apart: 20, of which 6 were waited for; matrix products, arithmetic and copies ran while one was open for 7% of the time, Pallas kernels for 0%

profile of v1, /device:TPU:0, one launch (start us, length us, event | category | flops | bytes accessed | tf_op | source)
XLA Modules:
  0.0 293.0 jit_solution(10155903407123012346)
XLA Ops:
  8.3 5.1 %collective-permute-start = (bf16[2,256,256]{2,1,0:T(8,128)(2,1)S(1)}, bf16[2,256,256]{2,1,0:T(8,128)(2,1)S(1)}, u32[]{:S(2)}, u32[]{:S(2)}) collective-permute-start(bf16[2,256,256]{2,1,0:T(8,128)(2,1)S(1)} %slice.68), channel_id=1, source_target_pairs={{0,3},{1,0},{2,1},{3,2},{4,7},{5,4},{6,5},{7,6},{8,11},{9,8},{10,9... | collective-permute-start | bytes 786440 | tf_op jit(solution)/shard_map/ppermute | solution.py:41
  13.4 1.6 slice.76
  15.0 3.8 %collective-permute-start.3 = (bf16[1,256,256]{2,1,0:T(8,128)(2,1)}, bf16[1,256,256]{2,1,0:T(8,128)(2,1)}, u32[]{:S(2)}, u32[]{:S(2)}) collective-permute-start(bf16[1,256,256]{2,1,0:T(8,128)(2,1)} %slice.76), channel_id=1, source_target_pairs={{0,3},{1,0},{2,1},{3,2},{4,7},{5,4},{6,5},{7,6},{8,11},{9,8},{10,9... | collective-permute-start | bytes 393224 | tf_op jit(solution)/shard_map/ppermute | solution.py:41
  18.8 3.8 %collective-permute-start.6 = (bf16[1,256,256]{2,1,0:T(8,128)(2,1)}, bf16[1,256,256]{2,1,0:T(8,128)(2,1)}, u32[]{:S(2)}, u32[]{:S(2)}) collective-permute-start(bf16[1,256,256]{2,1,0:T(8,128)(2,1)} %param.11), channel_id=1, source_target_pairs={{0,3},{1,0},{2,1},{3,2},{4,7},{5,4},{6,5},{7,6},{8,11},{9,8},{10,9... | collective-permute-start | bytes 393224 | tf_op jit(solution)/shard_map/ppermute | solution.py:41
  23.3 19.2 %all_gather.18 = bf16[2,1024,64]{1,2,0:T(8,128)(2,1)S(1)} all-gather(bf16[2,256,64]{1,2,0:T(8,128)(2,1)S(1)} %slice-done.1), channel_id=1, replica_groups=mesh['gz'=2,'row'=4,'col'=4] {'col'}, dimensions={1}, use_global_device_ids=true | all-gather | bytes 327680 | tf_op jit(solution)/shard_map/all_gather | solution.py:26
  44.1 2.2 collective-permute-start.7
  46.8 8.3 %collective-permute-done.2 = bf16[2,256,256]{2,1,0:T(8,128)(2,1)S(1)} collective-permute-done((bf16[2,256,256]{2,1,0:T(8,128)(2,1)S(1)}, bf16[2,256,256]{2,1,0:T(8,128)(2,1)S(1)}, u32[]{:S(2)}, u32[]{:S(2)}) %collective-permute-start.2) | collective-permute-done | bytes 262176 | tf_op jit(solution)/shard_map/ppermute | solution.py:39
  55.1 1.3 collective-permute-start.9
  58.0 30.0 %all-reduce.4.cloned.1.call-done = f32[1,256,64]{1,0,2:T(1,128)} async-done(((f32[1,256,64]{1,0,2:T(1,128)}), f32[1,256,64]{1,0,2:T(1,128)}) %all-reduce.4.cloned.1.call-update) | async-done | bytes 65552 | tf_op jit(solution)/shard_map/psum | solution.py:111
  88.9 13.5 %all_gather.19 = bf16[1,1024,64]{1,0,2:T(2,128)(2,1)S(1)} all-gather(bf16[1,256,64]{1,0,2:T(2,128)(2,1)S(1)} %fusion.43), channel_id=1, replica_groups=mesh['gz'=2,'row'=4,'col'=4] {'col'}, dimensions={1}, use_global_device_ids=true | all-gather | bytes 163840 | tf_op jit(solution)/shard_map/all_gather | solution.py:26
  102.9 1.0 convolution_add_fusion.14
  104.0 1.1 convolution_add_fusion.13
  105.0 7.7 %collective-permute-done.5 = bf16[1,256,256]{2,1,0:T(8,128)(2,1)S(1)} collective-permute-done((bf16[1,256,256]{2,1,0:T(8,128)(2,1)}, bf16[1,256,256]{2,1,0:T(8,128)(2,1)S(1)}, u32[]{:S(2)}, u32[]{:S(2)}) %collective-permute-start.5) | collective-permute-done | bytes 131104 | tf_op jit(solution)/shard_map/ppermute | solution.py:39
  114.1 51.9 %all-reduce.6.cloned.1.call-done = f32[1,256,64]{1,2,0:T(8,128)} async-done(((f32[1,256,64]{1,2,0:T(8,128)}), f32[1,256,64]{1,2,0:T(8,128)}) %all-reduce.6.cloned.1.call-update) | async-done | bytes 65552 | tf_op jit(solution)/shard_map/psum | solution.py:136
  166.9 13.4 %all_gather.20 = bf16[1,1024,64]{1,2,0:T(8,128)(2,1)S(1)} all-gather(bf16[1,256,64]{1,2,0:T(8,128)(2,1)S(1)} %subtract_convert_fusion), channel_id=1, replica_groups=mesh['gz'=2,'row'=4,'col'=4] {'col'}, dimensions={1}, use_global_device_ids=true | all-gather | bytes 163840 | tf_op jit(solution)/shard_map/all_gather | solution.py:26
  180.3 1.0 fusion.29
  181.3 1.5 collective-permute-start.13
  183.0 1.0 convolution_add_fusion.11
  184.0 1.1 convolution_add_fusion.10
  185.1 5.6 %collective-permute-done.8 = bf16[1,256,256]{2,1,0:T(8,128)(2,1)S(1)} collective-permute-done((bf16[1,256,256]{2,1,0:T(8,128)(2,1)}, bf16[1,256,256]{2,1,0:T(8,128)(2,1)S(1)}, u32[]{:S(2)}, u32[]{:S(2)}) %collective-permute-start.8) | collective-permute-done | bytes 131104 | tf_op jit(solution)/shard_map/ppermute | solution.py:39
  191.1 10.7 %psum.37 = bf16[1,256,64]{1,2,0:T(8,128)(2,1)S(1)} all-reduce(f32[1,256,64]{1,2,0:T(8,128)S(1)} %fusion.13), channel_id=1, replica_groups=mesh['gz'=2,'row'=4,'col'=4] {'row'}, use_global_device_ids=true, to_apply=%region_4.5 | all-reduce | flops 16384 | bytes 98304 | tf_op jit(solution)/shard_map/psum | solution.py:64
  201.8 14.4 %all_gather.21 = bf16[1,1024,64]{1,2,0:T(8,128)(2,1)S(1)} all-gather(bf16[1,256,64]{1,2,0:T(8,128)(2,1)S(1)} %psum.37), channel_id=1, replica_groups=mesh['gz'=2,'row'=4,'col'=4] {'col'}, dimensions={1}, use_global_device_ids=true | all-gather | bytes 163840 | tf_op jit(solution)/shard_map/all_gather | solution.py:26
  216.2 1.0 fusion.24
  217.3 3.1 %collective-permute-start.15 = (bf16[2,256,256]{2,1,0:T(8,128)(2,1)S(1)}, bf16[2,256,256]{2,1,0:T(8,128)(2,1)S(1)}, u32[]{:S(2)}, u32[]{:S(2)}) collective-permute-start(bf16[2,256,256]{2,1,0:T(8,128)(2,1)S(1)} %slice.87), channel_id=1, source_target_pairs={{0,3},{1,0},{2,1},{3,2},{4,7},{5,4},{6,5},{7,6},{8,11},{9,8},{10,9... | collective-permute-start | bytes 786440 | tf_op jit(solution)/shard_map/ppermute | solution.py:41
  221.7 1.1 convolution_add_fusion.7
  222.8 7.6 %collective-permute-done.11 = bf16[1,256,256]{2,1,0:T(8,128)(2,1)S(1)} collective-permute-done((bf16[1,256,256]{2,1,0:T(8,128)(2,1)}, bf16[1,256,256]{2,1,0:T(8,128)(2,1)S(1)}, u32[]{:S(2)}, u32[]{:S(2)}) %collective-permute-start.11) | collective-permute-done | bytes 131104 | tf_op jit(solution)/shard_map/ppermute | solution.py:39
  230.7 11.0 %psum.38 = bf16[1,256,64]{1,2,0:T(8,128)(2,1)S(1)} all-reduce(f32[1,256,64]{1,2,0:T(8,128)S(1)} %fusion.4), channel_id=1, replica_groups=mesh['gz'=2,'row'=4,'col'=4] {'row'}, use_global_device_ids=true, to_apply=%region_5.6 | all-reduce | flops 16384 | bytes 98304 | tf_op jit(solution)/shard_map/psum | solution.py:64
  241.6 13.4 %all_gather.22 = bf16[1,1024,64]{1,2,0:T(8,128)(2,1)S(1)} all-gather(bf16[1,256,64]{1,2,0:T(8,128)(2,1)S(1)} %psum.38), channel_id=1, replica_groups=mesh['gz'=2,'row'=4,'col'=4] {'col'}, dimensions={1}, use_global_device_ids=true | all-gather | bytes 163840 | tf_op jit(solution)/shard_map/all_gather | solution.py:26
  255.2 1.1 convolution_add_fusion.5
  256.4 1.1 convolution_add_fusion.3
  258.0 11.5 %all-reduce.7 = bf16[2,256,64]{1,2,0:T(8,128)(2,1)S(1)} all-reduce(f32[2,256,64]{1,2,0:T(8,128)S(1)} %bitcast_subtract_fusion), channel_id=1, replica_groups=mesh['gz'=2,'row'=4,'col'=4] {'row'}, use_global_device_ids=true, to_apply=%region_7.8 | all-reduce | flops 32768 | bytes 196608 | tf_op jit(solution)/shard_map/psum | solution.py:64
  269.5 14.2 %all_gather.23 = bf16[2,1024,64]{1,2,0:T(8,128)(2,1)S(1)} all-gather(bf16[2,256,64]{1,2,0:T(8,128)(2,1)S(1)} %all-reduce.7), channel_id=1, replica_groups=mesh['gz'=2,'row'=4,'col'=4] {'col'}, dimensions={1}, use_global_device_ids=true | all-gather | bytes 327680 | tf_op jit(solution)/shard_map/all_gather | solution.py:26
  (97 shorter events, 13.9 us)
Async XLA Ops:
  7.2 80.8 %all-reduce.4.cloned.1.call-start = ((), (), s32[]{:S(2)}) async-start(), calls=%async_computation | async-start | bytes 131072 | tf_op jit(solution)/shard_map/psum | solution.py:111
  7.2 15.4 %copy-start.5 = (s32[5,2]{0,1:T(2,128)S(1)}, s32[5,2]{0,1:T(2,128)}, u32[]{:S(2)}) copy-start(s32[5,2]{0,1:T(2,128)} %param.18) | copy-start | bytes 124
  7.2 15.5 %copy-start.6 = (s32[2]{0:T(128)S(1)}, s32[2]{0:T(128)}, u32[]{:S(2)}) copy-start(s32[2]{0:T(128)} %param.17) | copy-start | bytes 28
  7.2 16.1 %slice-start.1 = ((bf16[3,256,64]{1,2,0:T(8,128)(2,1)}), bf16[2,256,64]{1,2,0:T(8,128)(2,1)S(1)}, s32[]{:S(2)}) async-start(bf16[3,256,64]{1,2,0:T(8,128)(2,1)} %param.16), calls=%async_computation.3 | async-start | bytes 131072 | tf_op jit(solution)/shard_map/slice | solution.py:109
  8.2 35.0 %copy-start.2 = (bf16[8,256,256]{2,1,0:T(8,128)(2,1)S(1)}, bf16[8,256,256]{2,1,0:T(8,128)(2,1)}, u32[]{:S(2)}) copy-start(bf16[8,256,256]{2,1,0:T(8,128)(2,1)} %param.14) | copy-start | bytes 3145732
  8.3 35.9 %collective-permute-start = (bf16[2,256,256]{2,1,0:T(8,128)(2,1)S(1)}, bf16[2,256,256]{2,1,0:T(8,128)(2,1)S(1)}, u32[]{:S(2)}, u32[]{:S(2)}) collective-permute-start(bf16[2,256,256]{2,1,0:T(8,128)(2,1)S(1)} %slice.68), channel_id=1, source_target_pairs={{0,3},{1,0},{2,1},{3,2},{4,7},{5,4},{6,5},{7,6},{8,11},{9,8},{10,9... | collective-permute-start | bytes 786440 | tf_op jit(solution)/shard_map/ppermute | solution.py:41
  13.4 33.0 %collective-permute-start.1 = (bf16[2,256,256]{2,1,0:T(8,128)(2,1)S(1)}, bf16[2,256,256]{2,1,0:T(8,128)(2,1)S(1)}, u32[]{:S(2)}, u32[]{:S(2)}) collective-permute-start(bf16[2,256,256]{2,1,0:T(8,128)(2,1)S(1)} %slice.68), channel_id=1, source_target_pairs={{0,1},{1,2},{2,3},{3,0},{4,5},{5,6},{6,7},{7,4},{8,9},{9,10},{10,1... | collective-permute-start | bytes 786440 | tf_op jit(solution)/shard_map/ppermute | solution.py:39
  15.0 29.0 %copy-start = (bf16[8,256,256]{2,1,0:T(8,128)(2,1)S(1)}, bf16[8,256,256]{2,1,0:T(8,128)(2,1)}, u32[]{:S(2)}) copy-start(bf16[8,256,256]{2,1,0:T(8,128)(2,1)} %param.13) | copy-start | bytes 3145732
  15.0 87.8 %collective-permute-start.3 = (bf16[1,256,256]{2,1,0:T(8,128)(2,1)}, bf16[1,256,256]{2,1,0:T(8,128)(2,1)}, u32[]{:S(2)}, u32[]{:S(2)}) collective-permute-start(bf16[1,256,256]{2,1,0:T(8,128)(2,1)} %slice.76), channel_id=1, source_target_pairs={{0,3},{1,0},{2,1},{3,2},{4,7},{5,4},{6,5},{7,6},{8,11},{9,8},{10,9... | collective-permute-start | bytes 393224 | tf_op jit(solution)/shard_map/ppermute | solution.py:41
  18.8 84.0 %collective-permute-start.4 = (bf16[1,256,256]{2,1,0:T(8,128)(2,1)}, bf16[1,256,256]{2,1,0:T(8,128)(2,1)}, u32[]{:S(2)}, u32[]{:S(2)}) collective-permute-start(bf16[1,256,256]{2,1,0:T(8,128)(2,1)} %slice.76), channel_id=1, source_target_pairs={{0,1},{1,2},{2,3},{3,0},{4,5},{5,6},{6,7},{7,4},{8,9},{9,10},{10,1... | collective-permute-start | bytes 393224 | tf_op jit(solution)/shard_map/ppermute | solution.py:39
  18.8 162.6 %collective-permute-start.6 = (bf16[1,256,256]{2,1,0:T(8,128)(2,1)}, bf16[1,256,256]{2,1,0:T(8,128)(2,1)}, u32[]{:S(2)}, u32[]{:S(2)}) collective-permute-start(bf16[1,256,256]{2,1,0:T(8,128)(2,1)} %param.11), channel_id=1, source_target_pairs={{0,3},{1,0},{2,1},{3,2},{4,7},{5,4},{6,5},{7,6},{8,11},{9,8},{10,9... | collective-permute-start | bytes 393224 | tf_op jit(solution)/shard_map/ppermute | solution.py:41
  44.1 138.7 %collective-permute-start.7 = (bf16[1,256,256]{2,1,0:T(8,128)(2,1)}, bf16[1,256,256]{2,1,0:T(8,128)(2,1)}, u32[]{:S(2)}, u32[]{:S(2)}) collective-permute-start(bf16[1,256,256]{2,1,0:T(8,128)(2,1)} %param.11), channel_id=1, source_target_pairs={{0,1},{1,2},{2,3},{3,0},{4,5},{5,6},{6,7},{7,4},{8,9},{9,10},{10,1... | collective-permute-start | bytes 393224 | tf_op jit(solution)/shard_map/ppermute | solution.py:39
  46.4 8.7 %collective-permute-start.2 = (bf16[2,256,256]{2,1,0:T(8,128)(2,1)S(1)}, bf16[2,256,256]{2,1,0:T(8,128)(2,1)S(1)}, u32[]{:S(2)}, u32[]{:S(2)}) collective-permute-start(bf16[2,256,256]{2,1,0:T(8,128)(2,1)S(1)} %collective-permute-done.1), channel_id=1, source_target_pairs={{0,1},{1,2},{2,3},{3,0},{4,5},{5,6},{6,7},{7,4},{8,9},{9,10},{10,1... | collective-permute-start | bytes 786440 | tf_op jit(solution)/shard_map/ppermute | solution.py:39
  46.6 9.9 %slice-start = ((bf16[8,256,256]{2,1,0:T(8,128)(2,1)}), bf16[4,256,256]{2,1,0:T(8,128)(2,1)S(1)}, s32[]{:S(2)}) async-start(bf16[8,256,256]{2,1,0:T(8,128)(2,1)} %param.13), calls=%async_computation.2 | async-start | bytes 1048576 | tf_op jit(solution)/shard_map/slice | solution.py:116
  55.1 162.2 %collective-permute-start.9 = (bf16[1,256,256]{2,1,0:T(8,128)(2,1)}, bf16[1,256,256]{2,1,0:T(8,128)(2,1)S(1)}, u32[]{:S(2)}, u32[]{:S(2)}) collective-permute-start(bf16[1,256,256]{2,1,0:T(8,128)(2,1)} %param.12), channel_id=1, source_target_pairs={{0,3},{1,0},{2,1},{3,2},{4,7},{5,4},{6,5},{7,6},{8,11},{9,8},{10,9... | collective-permute-start | bytes 393224 | tf_op jit(solution)/shard_map/ppermute | solution.py:41
  56.3 0.7 copy-start.7
  56.5 46.1 %copy-start.1 = (bf16[8,256,256]{2,1,0:T(8,128)(2,1)S(1)}, bf16[8,256,256]{2,1,0:T(8,128)(2,1)}, u32[]{:S(2)}) copy-start(bf16[8,256,256]{2,1,0:T(8,128)(2,1)} %param.13) | copy-start | bytes 3145732
  57.9 30.1 %slice-start.2 = ((bf16[3,256,64]{1,2,0:T(8,128)(2,1)}), bf16[1,256,64]{1,2,0:T(8,128)(2,1)S(1)}, s32[]{:S(2)}) async-start(bf16[3,256,64]{1,2,0:T(8,128)(2,1)} %param.16), calls=%async_computation.4 | async-start | bytes 65536 | tf_op jit(solution)/shard_map/slice | solution.py:109
  57.9 108.1 %all-reduce.6.cloned.1.call-start = ((), (), s32[]{:S(2)}) async-start(), calls=%async_computation.1 | async-start | bytes 131072 | tf_op jit(solution)/shard_map/psum | solution.py:136
  102.8 117.5 %collective-permute-start.10 = (bf16[1,256,256]{2,1,0:T(8,128)(2,1)}, bf16[1,256,256]{2,1,0:T(8,128)(2,1)}, u32[]{:S(2)}, u32[]{:S(2)}) collective-permute-start(bf16[1,256,256]{2,1,0:T(8,128)(2,1)} %param.12), channel_id=1, source_target_pairs={{0,1},{1,2},{2,3},{3,0},{4,5},{5,6},{6,7},{7,4},{8,9},{9,10},{10,1... | collective-permute-start | bytes 393224 | tf_op jit(solution)/shard_map/ppermute | solution.py:39
  102.8 9.9 %collective-permute-start.5 = (bf16[1,256,256]{2,1,0:T(8,128)(2,1)}, bf16[1,256,256]{2,1,0:T(8,128)(2,1)S(1)}, u32[]{:S(2)}, u32[]{:S(2)}) collective-permute-start(bf16[1,256,256]{2,1,0:T(8,128)(2,1)} %collective-permute-done.4), channel_id=1, source_target_pairs={{0,1},{1,2},{2,3},{3,0},{4,5},{5,6},{6,7},{7,4},{8,9},{9,10},{10,1... | collective-permute-start | bytes 393224 | tf_op jit(solution)/shard_map/ppermute | solution.py:39
  103.9 8.8 %copy-start.3 = (bf16[1,256,256]{2,1,0:T(8,128)(2,1)S(1)}, bf16[1,256,256]{2,1,0:T(8,128)(2,1)}, u32[]{:S(2)}) copy-start(bf16[1,256,256]{2,1,0:T(8,128)(2,1)} %slice.82) | copy-start | bytes 393220
  112.7 142.5 %collective-permute-start.12 = (bf16[1,256,256]{2,1,0:T(8,128)(2,1)S(1)}, bf16[1,256,256]{2,1,0:T(8,128)(2,1)}, u32[]{:S(2)}, u32[]{:S(2)}) collective-permute-start(bf16[1,256,256]{2,1,0:T(8,128)(2,1)S(1)} %copy-done.3), channel_id=1, source_target_pairs={{0,3},{1,0},{2,1},{3,2},{4,7},{5,4},{6,5},{7,6},{8,11},{9,8},{10,9... | collective-permute-start | bytes 393224 | tf_op jit(solution)/shard_map/ppermute | solution.py:41
  113.9 52.1 %copy-start.4 = (bf16[1,256,64]{1,2,0:T(8,128)(2,1)S(1)}, bf16[1,256,64]{1,2,0:T(8,128)(2,1)}, u32[]{:S(2)}) copy-start(bf16[1,256,64]{1,2,0:T(8,128)(2,1)} %param.15) | copy-start | bytes 98308
  181.3 39.0 %collective-permute-start.13 = (bf16[1,256,256]{2,1,0:T(8,128)(2,1)S(1)}, bf16[1,256,256]{2,1,0:T(8,128)(2,1)S(1)}, u32[]{:S(2)}, u32[]{:S(2)}) collective-permute-start(bf16[1,256,256]{2,1,0:T(8,128)(2,1)S(1)} %copy-done.3), channel_id=1, source_target_pairs={{0,1},{1,2},{2,3},{3,0},{4,5},{5,6},{6,7},{7,4},{8,9},{9,10},{10,1... | collective-permute-start | bytes 393224 | tf_op jit(solution)/shard_map/ppermute | solution.py:39
  182.9 7.8 %collective-permute-start.8 = (bf16[1,256,256]{2,1,0:T(8,128)(2,1)}, bf16[1,256,256]{2,1,0:T(8,128)(2,1)S(1)}, u32[]{:S(2)}, u32[]{:S(2)}) collective-permute-start(bf16[1,256,256]{2,1,0:T(8,128)(2,1)} %collective-permute-done.7), channel_id=1, source_target_pairs={{0,1},{1,2},{2,3},{3,0},{4,5},{5,6},{6,7},{7,4},{8,9},{9,10},{10,1... | collective-permute-start | bytes 393224 | tf_op jit(solution)/shard_map/ppermute | solution.py:39
  190.7 29.9 %collective-permute-start.16 = (bf16[2,256,256]{2,1,0:T(8,128)(2,1)S(1)}, bf16[2,256,256]{2,1,0:T(8,128)(2,1)S(1)}, u32[]{:S(2)}, u32[]{:S(2)}) collective-permute-start(bf16[2,256,256]{2,1,0:T(8,128)(2,1)S(1)} %slice.87), channel_id=1, source_target_pairs={{0,1},{1,2},{2,3},{3,0},{4,5},{5,6},{6,7},{7,4},{8,9},{9,10},{10,1... | collective-permute-start | bytes 786440 | tf_op jit(solution)/shard_map/ppermute | solution.py:39
  217.3 66.9 %collective-permute-start.15 = (bf16[2,256,256]{2,1,0:T(8,128)(2,1)S(1)}, bf16[2,256,256]{2,1,0:T(8,128)(2,1)S(1)}, u32[]{:S(2)}, u32[]{:S(2)}) collective-permute-start(bf16[2,256,256]{2,1,0:T(8,128)(2,1)S(1)} %slice.87), channel_id=1, source_target_pairs={{0,3},{1,0},{2,1},{3,2},{4,7},{5,4},{6,5},{7,6},{8,11},{9,8},{10,9... | collective-permute-start | bytes 786440 | tf_op jit(solution)/shard_map/ppermute | solution.py:41
  220.3 10.0 %collective-permute-start.11 = (bf16[1,256,256]{2,1,0:T(8,128)(2,1)}, bf16[1,256,256]{2,1,0:T(8,128)(2,1)S(1)}, u32[]{:S(2)}, u32[]{:S(2)}) collective-permute-start(bf16[1,256,256]{2,1,0:T(8,128)(2,1)} %collective-permute-done.10), channel_id=1, source_target_pairs={{0,1},{1,2},{2,3},{3,0},{4,5},{5,6},{6,7},{7,4},{8,9},{9,10},{10,1... | collective-permute-start | bytes 393224 | tf_op jit(solution)/shard_map/ppermute | solution.py:39
  220.3 36.0 %collective-permute-start.14 = (bf16[1,256,256]{2,1,0:T(8,128)(2,1)S(1)}, bf16[1,256,256]{2,1,0:T(8,128)(2,1)}, u32[]{:S(2)}, u32[]{:S(2)}) collective-permute-start(bf16[1,256,256]{2,1,0:T(8,128)(2,1)S(1)} %collective-permute-done.13), channel_id=1, source_target_pairs={{0,1},{1,2},{2,3},{3,0},{4,5},{5,6},{6,7},{7,4},{8,9},{9,10},{10,1... | collective-permute-start | bytes 393224 | tf_op jit(solution)/shard_map/ppermute | solution.py:39
  220.5 63.8 %collective-permute-start.17 = (bf16[2,256,256]{2,1,0:T(8,128)(2,1)S(1)}, bf16[2,256,256]{2,1,0:T(8,128)(2,1)S(1)}, u32[]{:S(2)}, u32[]{:S(2)}) collective-permute-start(bf16[2,256,256]{2,1,0:T(8,128)(2,1)S(1)} %collective-permute-done.16), channel_id=1, source_target_pairs={{0,1},{1,2},{2,3},{3,0},{4,5},{5,6},{6,7},{7,4},{8,9},{9,10},{10,1... | collective-permute-start | bytes 786440 | tf_op jit(solution)/shard_map/ppermute | solution.py:39
Sparse Core Ops, SparseCore 0:
  58.0 29.9 all-reduce.3
  113.9 52.1 all-reduce.5
